TPU v7x, 256 devices: a whole 4x4x8 slice. The times are simulated.
256 devices in a mesh: replica: 16 (over z, core), mp: 16 (over y, x).
Axes of the slice: x: 4, y: 4, z: 8, core: 2. Of those that a mesh axis runs over, the one named last changes fastest.
Arguments:
- gradients: bfloat16 [16, 8, 768, 3072], P('replica', None, 'mp'), may hold values from -6 to 6
- feedback: bfloat16 [16, 8, 768, 3072], P('replica', None, 'mp'), may hold values from -4 to 4
- right_init: bfloat16 [8, 3072, 32], replicated, may hold values from -0.109375 to 0.109375
- gram_root: float32 [8, 32, 32], replicated, as said below
- owners: int32 [8], replicated, may hold values from 0 to 15, as said below
- momentum: float32 [16, 1, 768, 3072], P('mp', None, 'replica'), may hold values from -4 to 4
- master_weights: float32 [16, 1, 768, 3072], P('mp', None, 'replica'), may hold values from -1.5 to 1.5
- vector_grads: float32 [16, 10752], P('replica', 'mp'), may hold values from -6 to 6
- vector_momentum: float32 [10752], P('mp'), may hold values from -6 to 6
- vector_params: float32 [10752], P('mp'), may hold values from -6 to 6
Outputs:
- new_feedback: bfloat16 [16, 8, 768, 3072], P('replica', None, 'mp')
- new_momentum: float32 [16, 1, 768, 3072], P('mp', None, 'replica')
- new_master: float32 [16, 1, 768, 3072], P('mp', None, 'replica')
- new_weights: bfloat16 [8, 768, 3072], P(None, 'replica')
- new_vector_momentum: float32 [10752], P('mp')
- new_vector_params: float32 [10752], P('mp')
Inputs may be any that keep to these rules, and one draw needn't show every extreme that they name: `owners`: every matrix has one owner; no owner holds more than 1 of the 8 matrices, and one owner holds exactly 1. `gram_root`: each matrix is the identity plus off-diagonal terms, times a positive scale.
All inputs are finite; a program needn't handle non-finite values.
Results may differ from a plain program's by a relative error of at most 0.007.
Values may be sent and summed in bfloat16 or wider, within the bound.
A program may use at most 192 MiB of HBM per device.

v0:
```python
import jax
import jax.numpy as jnp
from jax import lax
from jax.sharding import PartitionSpec as P


def per_device(
    gradients,
    feedback,
    right_init,
    gram_root,
    owners,
    momentum,
    master_weights,
    vector_grads,
    vector_momentum,
    vector_params,
):
    highest = lax.Precision.HIGHEST
    compensated = (gradients[0].astype(jnp.float32) + feedback[0].astype(jnp.float32)).astype(
        jnp.bfloat16
    )
    owner_count = lax.axis_size("mp")
    capacity = momentum.shape[1]
    matrices = owners.shape[0]
    replica_rows = momentum.shape[2]
    mp_index = lax.axis_index("mp")
    replica_index = lax.axis_index("replica")
    same_owner = owners[:, None] == owners[None, :]
    earlier = jnp.arange(matrices)[:, None] < jnp.arange(matrices)[None, :]
    ranks = jnp.sum((same_owner & earlier).astype(jnp.int32), axis=0)
    slots = owners * capacity + ranks
    slot_table = (slots[None, :] == jnp.arange(owner_count * capacity)[:, None]).astype(jnp.float32)
    table_narrow = slot_table.astype(jnp.bfloat16)
    table_mine = lax.dynamic_slice_in_dim(slot_table, mp_index * capacity, capacity, 0)
    left_terms = jnp.einsum(
        "kmn,knr->kmr", compensated, right_init, preferred_element_type=jnp.float32
    )
    left_sum = lax.psum(left_terms, "replica")
    left_rows = jnp.einsum("kmr,krs->kms", left_sum, gram_root, precision=highest).astype(
        jnp.bfloat16
    )
    right_terms = jnp.einsum(
        "kmn,kms->kns", compensated, left_rows, preferred_element_type=jnp.float32
    )
    right_new = lax.psum(right_terms, ("replica", "mp"))
    left_all = lax.all_gather(left_rows, "mp", axis=1, tiled=True)
    approx_rows = jnp.einsum(
        "kms,kns->kmn", left_rows.astype(jnp.float32), right_new, precision=highest
    )
    new_feedback = (compensated.astype(jnp.float32) - approx_rows).astype(jnp.bfloat16)
    left_chosen = jnp.einsum(
        "ck,kmr->cmr", table_mine.astype(jnp.bfloat16), left_all, preferred_element_type=jnp.float32
    )
    left_chosen = lax.dynamic_slice_in_dim(
        left_chosen, replica_index * replica_rows, replica_rows, 1
    )
    right_chosen = jnp.einsum("ck,knr->cnr", table_mine, right_new, precision=highest)
    approx_slots = jnp.einsum("cmr,cnr->cmn", left_chosen, right_chosen, precision=highest)
    new_momentum = 0.9 * momentum[0] + approx_slots
    new_master = master_weights[0] - 0.1 * new_momentum
    master_narrow = new_master.astype(jnp.bfloat16)
    weight_slots = lax.all_gather(master_narrow, "mp", axis=0, tiled=True)
    new_weights = jnp.einsum(
        "sk,smn->kmn", table_narrow, weight_slots, preferred_element_type=jnp.float32
    ).astype(jnp.bfloat16)
    vector_total = lax.psum(vector_grads[0], "replica")
    new_vector_momentum = 0.9 * vector_momentum + vector_total
    new_vector_params = vector_params - 0.1 * new_vector_momentum
    return (
        new_feedback[None],
        new_momentum[None],
        new_master[None],
        new_weights,
        new_vector_momentum,
        new_vector_params,
    )


def solution(mesh):
    return jax.shard_map(
        per_device,
        mesh=mesh,
        in_specs=(
            P("replica", None, "mp", None),
            P("replica", None, "mp", None),
            P(),
            P(),
            P(),
            P("mp", None, "replica", None),
            P("mp", None, "replica", None),
            P("replica", "mp"),
            P("mp"),
            P("mp"),
        ),
        out_specs=(
            P("replica", None, "mp", None),
            P("mp", None, "replica", None),
            P("mp", None, "replica", None),
            P(None, "replica", None),
            P("mp"),
            P("mp"),
        ),
        check_vma=False,
    )
```

profile of v0, /device:TPU:1, one launch (start us, length us, event | category | flops | bytes accessed | tf_op | source)
XLA Modules:
  0.0 481.2 jit_solution(16211220204946410669)
XLA Ops:
  7.2 0.0 copy-start
  7.2 0.0 all-reduce.3.cloned.1.call-start
  7.2 0.8 reduce.1
  8.0 0.6 copy-done
  8.6 0.0 copy-start.5
  8.6 3.1 fusion.27
  11.8 50.5 %all-reduce = (f32[8,48,32]{1,2,0:T(8,128)S(1)}, f32[672]{0:T(1024)S(1)}) all-reduce(f32[8,48,32]{1,2,0:T(8,128)S(1)} %fusion.27, f32[672]{0:T(1024)S(1)} %reduce.1), channel_id=1, replica_groups=mesh['replica'=16,'mp'=16] {'replica'}, use_global_device_ids=true, to_apply=%region_0.0 | all-reduce | flops 12960 | bytes 103680 | tf_op jit(solution)/shard_map/psum | solution.py:39
  62.2 0.0 copy-done.5
  62.3 0.4 convolution_convert_fusion
  62.6 4.7 fusion.25
  67.3 0.0 copy-start.8
  67.3 0.0 all-reduce.3.cloned.1.call-update
  67.4 0.0 all-gather.3.cloned.1.call-start
  67.4 0.1 copy.26
  67.6 0.4 copy-done.8
  68.0 0.1 convert_reduce_fusion
  68.1 22.7 %all_gather.6 = bf16[8,768,32]{2,0,1:T(8,128)(2,1)S(1)} all-gather(bf16[8,48,32]{2,0,1:T(8,128)(2,1)S(1)} %copy.26), channel_id=1, replica_groups=mesh['replica'=16,'mp'=16] {'mp'}, dimensions={1}, use_global_device_ids=true | all-gather | bytes 417792 | tf_op jit(solution)/shard_map/all_gather | solution.py:47
  90.8 1.1 multiply_reduce_fusion
  91.9 239.2 %all-reduce.3.cloned.1.call-done = f32[8,3072,32]{1,2,0:T(8,128)} async-done(((f32[8,3072,32]{1,2,0:T(8,128)}), f32[8,3072,32]{1,2,0:T(8,128)}) %all-reduce.3.cloned.1.call-update) | async-done | bytes 3145744 | tf_op jit(solution)/shard_map/psum | solution.py:46
  331.1 44.7 %fusion.6 = f32[1,3072,32]{0,1,2:T(8,128)} fusion(f32[8,3072,32]{1,2,0:T(8,128)} %all-reduce.3.cloned.1.call-done, pred[16,8]{1,0:T(8,128)(4,1)S(1)} %get-tuple-element.31, s32[]{:T(128)S(6)} %select_n.6), kind=kOutput, calls=%fused_computation.7 | convolution fusion | flops 9437184 | bytes 3539460 | tf_op jit(solution)/shard_map/ck,knr->cnr/dot_general | solution.py:58
  375.7 0.0 copy-start.3
  375.7 0.0 copy-start.4
  375.7 27.1 %copy.35 = f32[1,3072,32]{1,2,0:T(8,128)S(1)} copy(f32[1,3072,32]{0,1,2:T(8,128)} %fusion.6) | data formatting | bytes 786432 | tf_op jit(solution)/shard_map/ck,knr->cnr/dot_general | solution.py:58
  402.9 0.0 copy-done.3
  402.9 0.0 copy-start.6
  402.9 0.0 copy-start.7
  402.9 0.6 convolution_add_fusion
  403.6 0.0 copy-done.4
  403.6 0.0 copy-start.2
  403.6 1.2 fusion.10
  404.7 0.0 all-gather.3.cloned.1.call-update
  404.8 0.0 copy-done.6
  404.8 0.0 copy-done.7
  404.8 0.6 multiply_subtract_fusion
  405.4 7.4 %fusion.5 = bf16[1,8,48,3072]{3,2,1,0:T(8,128)(2,1)} fusion(bf16[8,48,32]{1,2,0:T(8,128)(2,1)S(1)} %convolution_convert_fusion, f32[8,3072,32]{1,2,0:T(8,128)} %all-reduce.3.cloned.1.call-done, bf16[1,8,48,3072]{3,2,1,0:T(8,128)(2,1)} %param.11, bf16[1,8,48,3072]{3,2,1,0:T(8,128)(2,1)} %param.10), kind=kOutput, calls=%fused_computation.5 | convolution fusion | flops 461242368 | bytes 10248192 | tf_op jit(solution)/shard_map/kms,kns->kmn/dot_general | solution.py:48
  412.8 0.0 copy-done.2
  412.8 51.4 %all-gather.3.cloned.1.call-done = bf16[768,3072]{1,0:T(8,128)(2,1)} async-done(((bf16[48,3072]{1,0:T(8,128)(2,1)}), bf16[768,3072]{1,0:T(8,128)(2,1)}) %all-gather.3.cloned.1.call-update) | async-done | bytes 4718608 | tf_op jit(solution)/shard_map/all_gather | solution.py:63
  464.2 0.0 copy-start.1
  464.2 7.5 %fusion.2 = bf16[8,48,3072]{2,0,1:T(8,128)(2,1)S(1)} fusion(bf16[16,48,3072]{2,1,0:T(8,128)(2,1)} %bitcast.41, s32[8]{0:T(128)S(1)} %add.27), kind=kOutput, calls=%fused_computation.4 | convolution fusion | flops 38928768 | bytes 7077920 | tf_op jit(solution)/shard_map/sk,smn->kmn/dot_general | solution.py:64
  471.7 2.7 copy.29
  474.4 0.0 copy-done.1
  (3 shorter events, 0.0 us)
Async XLA Ops:
  7.2 1.4 copy-start
  7.2 323.9 %all-reduce.3.cloned.1.call-start = ((), (), s32[]{:S(2)}) async-start(), calls=%async_computation | async-start | bytes 6291456 | tf_op jit(solution)/shard_map/psum | solution.py:46
  8.6 53.6 %copy-start.5 = (f32[8,32,32]{2,1,0:T(8,128)S(1)}, f32[8,32,32]{2,1,0:T(8,128)}, u32[]{:S(2)}) copy-start(f32[8,32,32]{2,1,0:T(8,128)} %param.13) | copy-start | bytes 98308
  67.3 0.7 copy-start.8
  67.4 396.9 %all-gather.3.cloned.1.call-start = ((), (), s32[]{:S(2)}) async-start(), calls=%async_computation.1 | async-start | bytes 5013504 | tf_op jit(solution)/shard_map/all_gather | solution.py:63
  375.7 27.1 %copy-start.3 = (f32[1,1,48,3072]{3,2,1,0:T(8,128)S(1)}, f32[1,1,48,3072]{3,2,1,0:T(8,128)}, u32[]{:S(2)}) copy-start(f32[1,1,48,3072]{3,2,1,0:T(8,128)} %param.15) | copy-start | bytes 1769476
  375.7 27.8 %copy-start.4 = (f32[1,1,48,3072]{3,2,1,0:T(8,128)S(1)}, f32[1,1,48,3072]{3,2,1,0:T(8,128)}, u32[]{:S(2)}) copy-start(f32[1,1,48,3072]{3,2,1,0:T(8,128)} %param.16) | copy-start | bytes 1769476
  402.9 1.9 copy-start.6
  402.9 1.9 copy-start.7
  403.6 9.2 %copy-start.2 = (f32[48,3072]{1,0:T(8,128)}, f32[48,3072]{1,0:T(8,128)S(1)}, u32[]{:S(2)}) copy-start(f32[48,3072]{1,0:T(8,128)S(1)} %convolution_add_fusion) | copy-start | bytes 1769476
  464.2 10.2 %copy-start.1 = (bf16[8,3072,32]{1,2,0:T(8,128)(2,1)S(1)}, bf16[8,3072,32]{1,2,0:T(8,128)(2,1)}, u32[]{:S(2)}) copy-start(bf16[8,3072,32]{1,2,0:T(8,128)(2,1)} %param.12) | copy-start | bytes 4718596
Sparse Core Ops, SparseCore 0:
  67.5 263.5 all-reduce.2
  404.9 59.2 all-gather.2
where the time goes:
time: 482 us; the launch traced here: 481 us
  waiting for transfers between devices  291 us (60%)
  blocking collectives  73.2 us (15%)
  matrix products  68.4 us (14%)
  local copies, waits for them, and re-layouts  31 us (6%)
  between operations  14.2 us (3%)
    psum x1, waiting for transfers between devices, per_device(): right_new = lax.psum(right_terms, ('replica', 'mp'))  239 us
    all_gather x1, waiting for transfers between devices, per_device(): weight_slots = lax.all_gather(master_narrow, 'mp', axis=0, tiled=True)  51.4 us
    psum x1, blocking collectives, per_device(): left_sum = lax.psum(left_terms, 'replica')  50.5 us
    dot_general x1, matrix products, per_device(): jnp.einsum('ck,knr->cnr', table_mine, right_new, precision=highest)  44.7 us
    dot_general x1, local copies, waits for them, and re-layouts, per_device(): jnp.einsum('ck,knr->cnr', table_mine, right_new, precision=highest)  27.1 us
    all_gather x1, blocking collectives, per_device(): left_all = lax.all_gather(left_rows, 'mp', axis=1, tiled=True)  22.7 us
  transfers between devices with their start and end apart: 2, of which 2 were waited for; matrix products, arithmetic and copies ran while one was open for 2% of the time, Pallas kernels for 0%

commit v1 on v0

--- a/solution.py
+++ b/solution.py
@@ -60,7 +60,9 @@
     new_momentum = 0.9 * momentum[0] + approx_slots
     new_master = master_weights[0] - 0.1 * new_momentum
     master_narrow = new_master.astype(jnp.bfloat16)
-    weight_slots = lax.all_gather(master_narrow, "mp", axis=0, tiled=True)
+    weight_slots = jnp.concatenate(
+        lax.all_to_all(jnp.stack([master_narrow] * lax.axis_size("mp")), "mp", 0, 0), axis=0
+    )
     new_weights = jnp.einsum(
         "sk,smn->kmn", table_narrow, weight_slots, preferred_element_type=jnp.float32
     ).astype(jnp.bfloat16)

time: 482 us -> 504 us (1.046); the launches traced: 481 us -> 498 us
  waiting for transfers between devices: 291 us -> 298 us
  starting transfers between devices: 0.08 us -> 6.64 us
    all_to_all x0 -> x1, waiting for transfers between devices: none -> 58.8 us  [per_device(): lax.all_to_all(jnp.stack([master_narrow] * lax.axis_size('mp')), 'mp', 0, 0)]
    all_gather x1 -> x0, waiting for transfers between devices: 51.4 us -> none  [per_device(): weight_slots = lax.all_gather(master_narrow, 'mp', axis=0, tiled=True)]
    all_to_all x0 -> x1, starting transfers between devices: none -> 6.6 us  [per_device(): lax.all_to_all(jnp.stack([master_narrow] * lax.axis_size('mp')), 'mp', 0, 0)]
where the time goes in v1:
time: 504 us; the launch traced here: 498 us
  waiting for transfers between devices  298 us (59%)
  blocking collectives  73.4 us (15%)
  matrix products  68.5 us (14%)
  local copies, waits for them, and re-layouts  33.8 us (7%)
  between operations  14.2 us (3%)
  starting transfers between devices  6.64 us (1%)
    psum x1, waiting for transfers between devices, per_device(): right_new = lax.psum(right_terms, ('replica', 'mp'))  239 us
    all_to_all x1, waiting for transfers between devices, per_device(): lax.all_to_all(jnp.stack([master_narrow] * lax.axis_size('mp')), 'mp', 0, 0)  58.8 us
    psum x1, blocking collectives, per_device(): left_sum = lax.psum(left_terms, 'replica')  50.5 us
    dot_general x1, matrix products, per_device(): jnp.einsum('ck,knr->cnr', table_mine, right_new, precision=highest)  44.7 us
    dot_general x1, local copies, waits for them, and re-layouts, per_device(): jnp.einsum('ck,knr->cnr', table_mine, right_new, precision=highest)  27.1 us
    all_gather x1, blocking collectives, per_device(): left_all = lax.all_gather(left_rows, 'mp', axis=1, tiled=True)  23 us
  transfers between devices with their start and end apart: 2, of which 2 were waited for; matrix products, arithmetic and copies ran while one was open for 2% of the time, Pallas kernels for 0%

profile of v1, /device:TPU:1, one launch (start us, length us, event | category | flops | bytes accessed | tf_op | source)
XLA Modules:
  0.0 497.9 jit_solution(1466325815826389391)
XLA Ops:
  7.2 0.0 copy-start
  7.2 0.0 all-reduce.3.cloned.1.call-start
  7.2 0.8 reduce.1
  8.0 0.6 copy-done
  8.6 0.0 copy-start.5
  8.6 3.1 fusion.28
  11.8 50.5 %all-reduce = (f32[8,48,32]{1,2,0:T(8,128)S(1)}, f32[672]{0:T(1024)S(1)}) all-reduce(f32[8,48,32]{1,2,0:T(8,128)S(1)} %fusion.28, f32[672]{0:T(1024)S(1)} %reduce.1), channel_id=1, replica_groups=mesh['replica'=16,'mp'=16] {'replica'}, use_global_device_ids=true, to_apply=%region_0.0 | all-reduce | flops 12960 | bytes 103680 | tf_op jit(solution)/shard_map/psum | solution.py:39
  62.2 0.0 copy-done.5
  62.3 0.4 convolution_convert_fusion
  62.6 4.7 fusion.26
  67.4 0.0 copy-start.8
  67.4 0.0 all-reduce.3.cloned.1.call-update
  67.4 0.1 copy.25
  67.5 0.5 copy-done.8
  68.0 0.1 convert_reduce_fusion
  68.1 23.0 %all_gather.3 = bf16[8,768,32]{2,0,1:T(8,128)(2,1)S(1)} all-gather(bf16[8,48,32]{2,0,1:T(8,128)(2,1)S(1)} %copy.25), channel_id=1, replica_groups=mesh['replica'=16,'mp'=16] {'mp'}, dimensions={1}, use_global_device_ids=true | all-gather | bytes 417792 | tf_op jit(solution)/shard_map/all_gather | solution.py:47
  91.1 1.1 multiply_reduce_fusion
  92.2 238.8 %all-reduce.3.cloned.1.call-done = f32[8,3072,32]{1,2,0:T(8,128)} async-done(((f32[8,3072,32]{1,2,0:T(8,128)}), f32[8,3072,32]{1,2,0:T(8,128)}) %all-reduce.3.cloned.1.call-update) | async-done | bytes 3145744 | tf_op jit(solution)/shard_map/psum | solution.py:46
  331.0 44.7 %fusion.7 = f32[1,3072,32]{0,1,2:T(8,128)} fusion(f32[8,3072,32]{1,2,0:T(8,128)} %all-reduce.3.cloned.1.call-done, pred[16,8]{1,0:T(8,128)(4,1)S(1)} %get-tuple-element.31, s32[]{:T(128)S(6)} %select_n.6), kind=kOutput, calls=%fused_computation.8 | convolution fusion | flops 9437184 | bytes 3539460 | tf_op jit(solution)/shard_map/ck,knr->cnr/dot_general | solution.py:58
  375.8 0.0 copy-start.3
  375.8 0.0 copy-start.4
  375.8 27.1 %copy.34 = f32[1,3072,32]{1,2,0:T(8,128)S(1)} copy(f32[1,3072,32]{0,1,2:T(8,128)} %fusion.7) | data formatting | bytes 786432 | tf_op jit(solution)/shard_map/ck,knr->cnr/dot_general | solution.py:58
  402.9 0.0 copy-done.3
  402.9 0.6 convolution_add_fusion
  403.6 0.0 copy-done.4
  403.6 0.0 copy-start.2
  403.6 1.1 fusion.11
  404.6 2.8 stack.2
  407.4 0.0 copy-done.2
  407.4 0.0 copy-start.6
  407.4 0.0 copy-start.7
  407.4 6.6 %all-to-all-start = ((bf16[16,1,48,3072]{3,2,1,0:T(8,128)(2,1)}), bf16[16,1,48,3072]{3,2,1,0:T(8,128)(2,1)}, u32[]{:S(2)}, u32[]{:S(2)}) async-start(bf16[16,1,48,3072]{3,2,1,0:T(8,128)(2,1)} %stack.2), calls=%async_computation | async-start | bytes 9437184 | tf_op jit(solution)/shard_map/all_to_all | solution.py:64
  414.0 0.0 copy-done.6
  414.0 0.0 copy-done.7
  414.0 0.6 multiply_subtract_fusion
  414.6 7.4 %fusion.6 = bf16[1,8,48,3072]{3,2,1,0:T(8,128)(2,1)} fusion(bf16[8,48,32]{1,2,0:T(8,128)(2,1)S(1)} %convolution_convert_fusion, f32[8,3072,32]{1,2,0:T(8,128)} %all-reduce.3.cloned.1.call-done, bf16[1,8,48,3072]{3,2,1,0:T(8,128)(2,1)} %param.11, bf16[1,8,48,3072]{3,2,1,0:T(8,128)(2,1)} %param.10), kind=kOutput, calls=%fused_computation.6 | convolution fusion | flops 461242368 | bytes 10248192 | tf_op jit(solution)/shard_map/kms,kns->kmn/dot_general | solution.py:48
  422.0 58.8 %all-to-all-done = bf16[16,1,48,3072]{3,2,1,0:T(8,128)(2,1)} async-done(((bf16[16,1,48,3072]{3,2,1,0:T(8,128)(2,1)}), bf16[16,1,48,3072]{3,2,1,0:T(8,128)(2,1)}, u32[]{:S(2)}, u32[]{:S(2)}) %all-to-all-start) | async-done | bytes 4718624 | tf_op jit(solution)/shard_map/all_to_all | solution.py:64
  480.8 0.0 copy-start.1
  480.8 7.5 %fusion.3 = bf16[8,48,3072]{2,0,1:T(8,128)(2,1)S(1)} fusion(bf16[16,1,48,3072]{3,2,1,0:T(8,128)(2,1)} %all-to-all-done, s32[8]{0:T(128)S(1)} %add.27), kind=kOutput, calls=%fused_computation.5 | convolution fusion | flops 38928768 | bytes 7077920 | tf_op jit(solution)/shard_map/sk,smn->kmn/dot_general | solution.py:66
  488.3 2.7 copy.28
  491.0 0.0 copy-done.1
  (3 shorter events, 0.0 us)
Async XLA Ops:
  7.2 1.4 copy-start
  7.2 323.9 %all-reduce.3.cloned.1.call-start = ((), (), s32[]{:S(2)}) async-start(), calls=%async_computation.1 | async-start | bytes 6291456 | tf_op jit(solution)/shard_map/psum | solution.py:46
  8.6 53.6 %copy-start.5 = (f32[8,32,32]{2,1,0:T(8,128)S(1)}, f32[8,32,32]{2,1,0:T(8,128)}, u32[]{:S(2)}) copy-start(f32[8,32,32]{2,1,0:T(8,128)} %param.13) | copy-start | bytes 98308
  67.4 0.7 copy-start.8
  375.8 27.1 %copy-start.3 = (f32[1,1,48,3072]{3,2,1,0:T(8,128)S(1)}, f32[1,1,48,3072]{3,2,1,0:T(8,128)}, u32[]{:S(2)}) copy-start(f32[1,1,48,3072]{3,2,1,0:T(8,128)} %param.15) | copy-start | bytes 1769476
  375.8 27.8 %copy-start.4 = (f32[1,1,48,3072]{3,2,1,0:T(8,128)S(1)}, f32[1,1,48,3072]{3,2,1,0:T(8,128)}, u32[]{:S(2)}) copy-start(f32[1,1,48,3072]{3,2,1,0:T(8,128)} %param.16) | copy-start | bytes 1769476
  403.6 3.8 copy-start.2
  407.4 6.6 %copy-start.6 = (f32[672]{0:T(1024)S(1)}, f32[672]{0:T(1024)}, u32[]{:S(2)}) copy-start(f32[672]{0:T(1024)} %param.19) | copy-start | bytes 8068
  407.4 6.6 %copy-start.7 = (f32[672]{0:T(1024)S(1)}, f32[672]{0:T(1024)}, u32[]{:S(2)}) copy-start(f32[672]{0:T(1024)} %param.18) | copy-start | bytes 8068
  407.4 73.4 %all-to-all-start = ((bf16[16,1,48,3072]{3,2,1,0:T(8,128)(2,1)}), bf16[16,1,48,3072]{3,2,1,0:T(8,128)(2,1)}, u32[]{:S(2)}, u32[]{:S(2)}) async-start(bf16[16,1,48,3072]{3,2,1,0:T(8,128)(2,1)} %stack.2), calls=%async_computation | async-start | bytes 9437184 | tf_op jit(solution)/shard_map/all_to_all | solution.py:64
  480.8 10.2 %copy-start.1 = (bf16[8,3072,32]{1,2,0:T(8,128)(2,1)S(1)}, bf16[8,3072,32]{1,2,0:T(8,128)(2,1)}, u32[]{:S(2)}) copy-start(bf16[8,3072,32]{1,2,0:T(8,128)(2,1)} %param.12) | copy-start | bytes 4718596
Sparse Core Ops, SparseCore 0:
  67.5 263.4 all-reduce.2
